TPU v7x, 512 devices: a whole 4x4x16 slice. The times are simulated.
512 devices in a mesh: row: 16 (over z_hi, y, core), col: 32 (over z_lo, x).
Axes of the slice: x: 4, y: 4, z: 16 (z_hi: 2, z_lo: 8; z = z_hi * 8 + z_lo), core: 2. Of those that a mesh axis runs over, the one named last changes fastest.
Arguments:
- tokens: bfloat16 [256, 8192], P('col', 'row'), may hold values from -6 to 6
- up_blocks: bfloat16 [16, 32, 7, 128, 128], P('row', 'col'), may hold values from -0.1875 to 0.1875
- up_index: int32 [16, 32, 7], P('row', 'col'), may hold values from 0 to 28, as said below
- down_blocks: bfloat16 [16, 32, 7, 128, 128], P('row', 'col'), may hold values from -0.09375 to 0.09375
- down_index: int32 [16, 32, 7], P('row', 'col'), may hold values from 0 to 28, as said below
- out_cot: bfloat16 [256, 8192], P('col', 'row'), may hold values from -1.5 to 1.5
Outputs:
- outputs: bfloat16 [256, 8192], P('col', 'row')
- input_grad: bfloat16 [256, 8192], P('col', 'row')
- up_grad: bfloat16 [16, 32, 7, 128, 128], P('row', 'col')
- down_grad: bfloat16 [16, 32, 7, 128, 128], P('row', 'col')
Inputs may be any that keep to these rules, and one draw needn't show every extreme that they name: `up_index`: each entry names a block of its tile's 4 x 7 grid as row * 7 + column, or is 28 for an empty slot; the named blocks of a tile are distinct and come before its empty slots; every tile names at least one block; the tiles (r, c) with c * 16 // 32 == r name 7 blocks, every other tile fewer. `down_index`: each entry names a block of its tile's 7 x 4 grid (hidden-unit block, width block) as row * 4 + column, or is 28 for an empty slot; the named blocks of a tile are distinct and come before its empty slots; every tile names at least one block; the tiles (r, c) with c * 16 // 32 == r name 7 blocks, every other tile fewer.
All inputs are finite; a program needn't handle non-finite values.
Results may differ from a plain program's by a relative error of at most 0.023.
Values may be sent and summed in bfloat16 or wider, within the bound.
A program may use at most 64 MiB of HBM per device.

v0:
```python
import jax
import jax.numpy as jnp
from jax import lax
from jax.sharding import PartitionSpec as P

FF = 28672
BS = 128


COEF = 0.7978845608
CUBIC = 0.044715


def gelu_value(values):
    inner = COEF * (values + CUBIC * values * values * values)
    return 0.5 * values * (1.0 + jnp.tanh(inner))


def gelu_slope(values):
    tangent = jnp.tanh(COEF * (values + CUBIC * values * values * values))
    return 0.5 * (1.0 + tangent) + 0.5 * values * (1.0 - tangent * tangent) * COEF * (
        1.0 + 3.0 * CUBIC * values * values
    )


def selectors(indices, leading, trailing):
    lead_pos = indices // trailing
    trail_pos = indices % trailing
    valid = indices < leading * trailing
    lead_sel = (lead_pos[:, None] == jnp.arange(leading, dtype=jnp.int32)[None, :]).astype(
        jnp.bfloat16
    )
    trail_sel = (trail_pos[:, None] == jnp.arange(trailing, dtype=jnp.int32)[None, :]).astype(
        jnp.bfloat16
    )
    return (indices, lead_pos, trail_pos, valid, lead_sel, trail_sel)


def place_blocks(products, positions, valid, width_blocks):
    tok_count = products.shape[0]
    masked = products * valid.astype(jnp.float32)[None, :, None]
    clipped = jnp.clip(positions, 0, width_blocks - 1)
    result = jnp.zeros((tok_count, width_blocks, BS), jnp.float32).at[:, clipped, :].add(masked)
    return result.reshape(tok_count, width_blocks * BS)


def forward_tile(operand, blocks, pattern):
    indices, lead_pos, trail_pos, valid, lead_sel, trail_sel = pattern
    tok_count = operand.shape[0]
    pieces = operand.reshape(tok_count, lead_sel.shape[1], BS)
    picked = jnp.einsum("tab,ka->ktb", pieces, lead_sel, preferred_element_type=jnp.float32).astype(
        jnp.bfloat16
    )
    products = jnp.einsum("ktb,kbd->tkd", picked, blocks, preferred_element_type=jnp.float32)
    return place_blocks(products, trail_pos, valid, trail_sel.shape[1])


def backward_tile(other, blocks, pattern):
    indices, lead_pos, trail_pos, valid, lead_sel, trail_sel = pattern
    tok_count = other.shape[0]
    pieces = other.reshape(tok_count, trail_sel.shape[1], BS)
    picked = jnp.einsum(
        "tcd,kc->ktd", pieces, trail_sel, preferred_element_type=jnp.float32
    ).astype(jnp.bfloat16)
    products = jnp.einsum("ktd,kbd->tkb", picked, blocks, preferred_element_type=jnp.float32)
    return place_blocks(products, lead_pos, valid, lead_sel.shape[1])


def grad_tile(operand, other, pattern):
    indices, lead_pos, trail_pos, valid, lead_sel, trail_sel = pattern
    tok_count = operand.shape[0]
    leading = lead_sel.shape[1]
    trailing = trail_sel.shape[1]
    left_pick = jnp.einsum(
        "tab,ka->ktb",
        operand.reshape(tok_count, leading, BS),
        lead_sel,
        preferred_element_type=jnp.float32,
    ).astype(jnp.bfloat16)
    right_pick = jnp.einsum(
        "tcd,kc->ktd",
        other.reshape(tok_count, trailing, BS),
        trail_sel,
        preferred_element_type=jnp.float32,
    ).astype(jnp.bfloat16)
    return jnp.einsum("ktb,ktd->kbd", left_pick, right_pick, preferred_element_type=jnp.float32)


def shards(tokens, up_blocks, up_index, down_blocks, down_index, out_cot):
    row_blocks = tokens.shape[1] // BS
    col_blocks = FF // (BS * lax.axis_size("col"))
    row_devices = lax.axis_size("row")
    up_weight = up_blocks[0, 0]
    down_weight = down_blocks[0, 0]
    up_pattern = selectors(up_index[0, 0], row_blocks, col_blocks)
    down_pattern = selectors(down_index[0, 0], col_blocks, row_blocks)
    features = lax.all_gather(tokens, "col", axis=0, tiled=True)
    partial_value = forward_tile(features, up_weight, up_pattern)
    tok_count = partial_value.shape[0]
    share_rows = tok_count // row_devices
    hidden_width = partial_value.shape[1]
    received = lax.all_to_all(
        partial_value.astype(jnp.bfloat16).reshape(row_devices, share_rows, hidden_width),
        "row",
        split_axis=0,
        concat_axis=0,
        tiled=True,
    )
    pre_share = jnp.sum(received.astype(jnp.float32), axis=0)
    preact = lax.all_gather(pre_share.astype(jnp.bfloat16), "row", axis=0, tiled=True).astype(
        pre_share.dtype
    )
    hidden = gelu_value(preact).astype(jnp.bfloat16)
    out_terms = forward_tile(hidden, down_weight, down_pattern)
    outputs = lax.psum_scatter(
        out_terms.astype(jnp.bfloat16), "col", scatter_dimension=0, tiled=True
    )
    cotangents = lax.all_gather(out_cot, "col", axis=0, tiled=True)
    act_terms = backward_tile(cotangents, down_weight, down_pattern)
    act_received = lax.all_to_all(
        act_terms.astype(jnp.bfloat16).reshape(row_devices, share_rows, hidden_width),
        "row",
        split_axis=0,
        concat_axis=0,
        tiled=True,
    )
    act_share = jnp.sum(act_received.astype(jnp.float32), axis=0)
    act_grad = lax.all_gather(act_share.astype(jnp.bfloat16), "row", axis=0, tiled=True).astype(
        act_share.dtype
    )
    pre_grad = (act_grad * gelu_slope(preact)).astype(jnp.bfloat16)
    input_terms = backward_tile(pre_grad, up_weight, up_pattern)
    input_grad = lax.psum_scatter(
        input_terms.astype(jnp.bfloat16), "col", scatter_dimension=0, tiled=True
    )
    up_grad = grad_tile(features, pre_grad, up_pattern).astype(jnp.bfloat16)
    down_grad = grad_tile(hidden, cotangents, down_pattern).astype(jnp.bfloat16)
    return (outputs, input_grad, up_grad[None, None], down_grad[None, None])


def solution(mesh):
    placed = (
        P("col", "row"),
        P("row", "col", None, None, None),
        P("row", "col", None),
        P("row", "col", None, None, None),
        P("row", "col", None),
        P("col", "row"),
    )
    return jax.shard_map(
        shards,
        mesh=mesh,
        in_specs=placed,
        out_specs=(
            P("col", "row"),
            P("col", "row"),
            P("row", "col", None, None, None),
            P("row", "col", None, None, None),
        ),
        check_vma=False,
    )
```

profile of v0, /device:TPU:8, one launch (start us, length us, event | category | flops | bytes accessed | tf_op | source)
XLA Modules:
  0.0 847.9 jit_solution(4409887244317478387)
XLA Ops:
  7.2 0.7 fusion.40
  8.0 128.2 %all_gather.12 = bf16[256,512]{1,0:T(8,128)(2,1)S(1)} all-gather(bf16[8,512]{1,0:T(8,128)(2,1)} %param.6), channel_id=1, replica_groups=mesh['row'=16,'col'=32] {'col'}, dimensions={0}, use_global_device_ids=true | all-gather | bytes 270336 | tf_op jit(solution)/shard_map/all_gather | solution.py:97
  136.1 0.1 reshape.301
  136.2 0.3 fusion.26
  136.6 0.3 convolution_multiply_fusion.3
  136.9 1.4 scatter_fusion
  138.3 0.1 convert_element_type.90
  138.4 0.3 copy.53
  138.7 1.3 convert_element_type.91
  140.0 13.0 %all-to-all-start = ((bf16[16,16,896]{2,1,0:T(8,128)(2,1)}), bf16[16,16,896]{2,1,0:T(8,128)(2,1)}, u32[]{:S(2)}, u32[]{:S(2)}) async-start(bf16[16,16,896]{2,1,0:T(8,128)(2,1)} %convert_element_type.91), calls=%async_computation | async-start | bytes 917504 | tf_op jit(solution)/shard_map/all_to_all | solution.py:102
  153.0 117.5 %all_gather.14 = bf16[256,512]{1,0:T(8,128)(2,1)S(1)} all-gather(bf16[8,512]{1,0:T(8,128)(2,1)S(1)} %copy-done.7), channel_id=1, replica_groups=mesh['row'=16,'col'=32] {'col'}, dimensions={0}, use_global_device_ids=true | all-gather | bytes 270336 | tf_op jit(solution)/shard_map/all_gather | solution.py:118
  270.5 0.1 reshape.303
  270.5 0.6 copy-done.9
  271.2 0.3 fusion.29
  271.5 0.6 copy-done.6
  272.1 0.3 convolution_multiply_fusion.1
  272.5 1.4 scatter_fusion.2
  273.8 0.1 convert_element_type.99
  273.9 0.3 copy.59
  274.2 1.3 convert_element_type.100
  275.5 14.0 %all-to-all-start.1 = ((bf16[16,16,896]{2,1,0:T(8,128)(2,1)}), bf16[16,16,896]{2,1,0:T(8,128)(2,1)S(1)}, u32[]{:S(2)}, u32[]{:S(2)}) async-start(bf16[16,16,896]{2,1,0:T(8,128)(2,1)} %convert_element_type.100), calls=%async_computation.1 | async-start | bytes 917504 | tf_op jit(solution)/shard_map/all_to_all | solution.py:120
  289.5 1.1 reduce_sum.24
  290.6 39.3 %all_gather.13 = bf16[256,896]{1,0:T(8,128)(2,1)S(1)} all-gather(bf16[16,896]{1,0:T(8,128)(2,1)S(1)} %reduce_sum.24), channel_id=1, replica_groups=mesh['row'=16,'col'=32] {'row'}, dimensions={0}, use_global_device_ids=true | all-gather | bytes 487424 | tf_op jit(solution)/shard_map/all_gather | solution.py:110
  329.9 0.2 copy.54
  330.2 0.1 reduce_sum.25
  330.2 42.8 %all_gather.15 = bf16[256,896]{1,0:T(8,128)(2,1)S(1)} all-gather(bf16[16,896]{1,0:T(8,128)(2,1)S(1)} %reduce_sum.25), channel_id=1, replica_groups=mesh['row'=16,'col'=32] {'row'}, dimensions={0}, use_global_device_ids=true | all-gather | bytes 487424 | tf_op jit(solution)/shard_map/all_gather | solution.py:128
  373.0 0.2 copy.60
  373.2 1.5 fusion.9
  374.7 0.3 copy.61
  375.0 0.4 fusion.21
  375.4 0.3 convolution_multiply_fusion
  375.7 0.5 copy-done.1
  376.2 1.4 scatter_fusion.3
  377.6 0.1 copy.63
  377.7 0.9 copy.72
  378.7 0.1 copy-done.5
  378.8 0.3 copy.55
  379.1 0.4 fusion.18
  379.4 0.3 convolution_multiply_fusion.2
  379.7 0.5 copy-done.3
  380.3 1.4 scatter_fusion.1
  381.7 0.1 copy.57
  381.8 0.9 copy.70
  382.7 0.1 copy-done.2
  382.9 1.0 fusion
  383.9 1.0 fusion.1
  384.9 221.5 %reduce-scatter.9.cloned.1.call-done = bf16[8,512]{1,0:T(8,128)(2,1)} async-done(((bf16[256,512]{1,0:T(8,128)(2,1)}), bf16[8,512]{1,0:T(8,128)(2,1)}) %reduce-scatter.9.cloned.1.call-update) | async-done | bytes 8208
  606.4 234.7 %reduce-scatter.7.cloned.1.call-done = bf16[8,512]{1,0:T(8,128)(2,1)} async-done(((bf16[256,512]{1,0:T(8,128)(2,1)}), bf16[8,512]{1,0:T(8,128)(2,1)}) %reduce-scatter.7.cloned.1.call-update) | async-done | bytes 8208
  (31 shorter events, 0.5 us)
Async XLA Ops:
  7.2 129.4 %copy-start = (bf16[1,1,7,128,128]{4,3,2,1,0:T(8,128)(2,1)S(1)}, bf16[1,1,7,128,128]{4,3,2,1,0:T(8,128)(2,1)}, u32[]{:S(2)}) copy-start(bf16[1,1,7,128,128]{4,3,2,1,0:T(8,128)(2,1)} %param.7) | copy-start | bytes 688132
  7.2 0.8 copy-start.8
  140.0 13.0 %copy-start.7 = (bf16[8,512]{1,0:T(8,128)(2,1)S(1)}, bf16[8,512]{1,0:T(8,128)(2,1)}, u32[]{:S(2)}) copy-start(bf16[8,512]{1,0:T(8,128)(2,1)} %param.11) | copy-start | bytes 24580
  140.0 135.5 %all-to-all-start = ((bf16[16,16,896]{2,1,0:T(8,128)(2,1)}), bf16[16,16,896]{2,1,0:T(8,128)(2,1)}, u32[]{:S(2)}, u32[]{:S(2)}) async-start(bf16[16,16,896]{2,1,0:T(8,128)(2,1)} %convert_element_type.91), calls=%async_computation | async-start | bytes 917504 | tf_op jit(solution)/shard_map/all_to_all | solution.py:102
  270.5 0.7 copy-start.9
  271.2 0.9 copy-start.6
  275.5 54.6 %all-to-all-start.1 = ((bf16[16,16,896]{2,1,0:T(8,128)(2,1)}), bf16[16,16,896]{2,1,0:T(8,128)(2,1)S(1)}, u32[]{:S(2)}, u32[]{:S(2)}) async-start(bf16[16,16,896]{2,1,0:T(8,128)(2,1)} %convert_element_type.100), calls=%async_computation.1 | async-start | bytes 917504 | tf_op jit(solution)/shard_map/all_to_all | solution.py:120
  289.5 316.9 %reduce-scatter.9.cloned.1.call-start = ((), (), s32[]{:S(2)}) async-start(), calls=%async_computation.5 | async-start | bytes 270336
  375.3 0.8 copy-start.1
  377.7 1.0 copy-start.5
  378.6 462.5 %reduce-scatter.7.cloned.1.call-start = ((), (), s32[]{:S(2)}) async-start(), calls=%async_computation.4 | async-start | bytes 270336
  379.4 0.8 copy-start.3
  381.8 1.0 copy-start.2
  382.9 1.0 copy-start.4
Sparse Core Ops, SparseCore 0:
  378.8 227.6 reduce-scatter.8
  610.0 231.0 reduce-scatter.6
where the time goes:
time: 849 us; the launch traced here: 848 us
  waiting for transfers between devices  456 us (54%)
  blocking collectives  328 us (39%)
  starting transfers between devices  27 us (3%)
  between operations  14.4 us (2%)
  other arithmetic  9.06 us (1%)
  local copies, waits for them, and re-layouts  9.03 us (1%)
    unnamed x4, waiting for transfers between devices  456 us
    all_gather x1, blocking collectives, shards(): features = lax.all_gather(tokens, 'col', axis=0, tiled=True)  128 us
    all_gather x1, blocking collectives, shards(): cotangents = lax.all_gather(out_cot, 'col', axis=0, tiled=True)  117 us
    all_gather x1, blocking collectives, shards(): lax.all_gather(act_share.astype(jnp.bfloat16), 'row', axis=0, tiled=True)  42.8 us
    all_gather x1, blocking collectives, shards(): lax.all_gather(pre_share.astype(jnp.bfloat16), 'row', axis=0, tiled=True)  39.3 us
  transfers between devices with their start and end apart: 4, of which 2 were waited for; matrix products, arithmetic and copies ran while one was open for 1% of the time, Pallas kernels for 0%

commit v1 on v0

v1 whole, which is shorter than its diff:
```python
import functools

import jax
import jax.numpy as jnp
from jax import lax
from jax.experimental import pallas as pl
from jax.experimental.pallas import tpu as pltpu
from jax.sharding import PartitionSpec as P

MESH = pl.DeviceIdType.MESH
BF16 = jnp.bfloat16
F32 = jnp.float32

BS = 128
NX = 4
NY = 4
NC = 2

COEF = 0.7978845608
CUBIC = 0.044715


def body(
    dims,
    tok_ref,
    cot_ref,
    up_idx,
    down_idx,
    up_hbm,
    down_hbm,
    out_ref,
    ing_ref,
    upg_hbm,
    downg_hbm,
    up_blk,
    down_blk,
    w1,
    w2,
    tok_all,
    cot_all,
    feats,
    cots,
    term,
    r1,
    half,
    r2,
    share,
    r3,
    hid,
    xterm,
    e1,
    zsum,
    e2,
    gdense,
    gout,
    local_sem,
    send_sem,
    recv_sem,
):
    nz, nx, nzh, ny, nc, rb, cb, slots = dims
    row = lax.axis_index("row")
    col = lax.axis_index("col")
    core = row % nc
    y = (row // nc) % ny
    zh = row // (nc * ny)
    x = col % nx
    z = col // nx
    tok_count = nz * nx * tok_ref.shape[0]
    wide = rb * BS
    tall = cb * BS

    def row_of(zh_, y_, core_):
        return (zh_ * ny + y_) * nc + core_

    def z_dev(k):
        return (row, ((z + k) % nz) * nx + x)

    def x_dev(k):
        return (row, z * nx + (x + k) % nx)

    def y_dev(k):
        return (row_of(zh, (y + k) % ny, core), col)

    core_dev = (row_of(zh, y, 1 - core), col)
    zh_dev = (row_of(1 - zh, y, core), col)

    partners = [z_dev(k) for k in range(1, nz)] + [x_dev(k) for k in range(1, nx)]
    partners += [y_dev(k) for k in range(1, ny)] + [core_dev, zh_dev]

    count = [0]
    started = []

    def send(src, dst, device):
        at = count[0]
        count[0] += 1
        copy = pltpu.make_async_remote_copy(
            src_ref=src,
            dst_ref=dst,
            send_sem=send_sem.at[at],
            recv_sem=recv_sem.at[at],
            device_id=device,
            device_id_type=MESH,
        )
        copy.start()
        started.append(copy)
        return copy

    up_load = pltpu.make_async_copy(up_hbm.at[0, 0], up_blk.at[pl.ds(0, slots)], local_sem.at[0])
    down_load = pltpu.make_async_copy(
        down_hbm.at[0, 0], down_blk.at[pl.ds(0, slots)], local_sem.at[1]
    )
    up_load.start()
    down_load.start()

    barrier = pltpu.get_barrier_semaphore()
    for device in partners:
        pl.semaphore_signal(barrier, inc=1, device_id=device, device_id_type=MESH)
    pl.semaphore_wait(barrier, len(partners))

    gather_z = []
    for own, full in ((tok_ref, tok_all), (cot_ref, cot_all)):
        gather_z.append([send(own, full.at[0, k], z_dev(k)) for k in range(1, nz)])
        full[0, 0] = own[...]

    for load, blk, index, dense, leading, trailing in (
        (up_load, up_blk, up_idx, w1, rb, cb),
        (down_load, down_blk, down_idx, w2, cb, rb),
    ):
        blk[slots] = jnp.zeros((BS, BS), BF16)
        load.wait()
        entries = [index[0, 0, k] for k in range(slots)]
        for place in range(leading * trailing):
            slot = jnp.int32(slots)
            for k in range(slots):
                slot = jnp.where(entries[k] == place, jnp.int32(k), slot)
            a, b = place // trailing, place % trailing
            dense[a * BS : (a + 1) * BS, b * BS : (b + 1) * BS] = blk[slot]

    gather_x = []
    for copies, full in zip(gather_z, (tok_all, cot_all)):
        for copy in copies:
            copy.wait_recv()
        gather_x.append([send(full.at[0], full.at[k], x_dev(k)) for k in range(1, nx)])

    per_x = tok_count // nx
    parts = nc * ny
    rows = tok_count // parts
    to_core = []
    for s, (copies, full, flat) in enumerate(
        zip(gather_x, (tok_all, cot_all), (feats, cots))
    ):
        for copy in copies:
            copy.wait_recv()
        for k in range(nx):
            flat[k * per_x : (k + 1) * per_x, :] = (
                full[k].astype(F32).reshape(per_x, wide).astype(BF16)
            )
        if s == 0:
            value = jnp.dot(flat[...], w1[...], preferred_element_type=F32)
        else:
            value = lax.dot_general(
                flat[...], w2[...], (((1,), (1,)), ((), ())), preferred_element_type=F32
            )
        term[s] = value.astype(BF16).reshape(parts, rows, tall)
        to_core.append(
            send(term.at[s, pl.ds((1 - core) * ny, ny)], r1.at[s], core_dev)
        )

    to_y = []
    for s in range(2):
        to_core[s].wait_recv()
        half[s] = (
            term[s, pl.ds(core * ny, ny)].astype(F32) + r1[s].astype(F32)
        ).astype(BF16)
        to_y.append(
            [send(half.at[s, (y + k) % ny], r2.at[s, k - 1], y_dev(k)) for k in range(1, ny)]
        )
    to_zh = []
    for s in range(2):
        for copy in to_y[s]:
            copy.wait_recv()
        total = half[s, y].astype(F32)
        for k in range(1, ny):
            total = total + r2[s, k - 1].astype(F32)
        share[s] = total.astype(BF16)
        to_zh.append(send(share.at[s], r3.at[s], zh_dev))

    mine = core * ny + y
    to_zh[0].wait_recv()
    v = share[0].astype(F32) + r3[0].astype(F32)
    t = jnp.tanh(COEF * (v + CUBIC * v * v * v))
    hid[0, mine] = (0.5 * v * (1.0 + t)).astype(BF16)
    spread_y = [[send(hid.at[0, mine], hid.at[0, mine], y_dev(k)) for k in range(1, ny)]]
    slope = 0.5 * (1.0 + t) + 0.5 * v * (1.0 - t * t) * COEF * (1.0 + 3.0 * CUBIC * v * v)
    to_zh[1].wait_recv()
    act = share[1].astype(F32) + r3[1].astype(F32)
    hid[1, mine] = (act * slope).astype(BF16)
    spread_y.append([send(hid.at[1, mine], hid.at[1, mine], y_dev(k)) for k in range(1, ny)])
    spread_core = []
    for s in range(2):
        for copy in spread_y[s]:
            copy.wait_recv()
        mine_half = pl.ds(core * ny, ny)
        spread_core.append(send(hid.at[s, mine_half], hid.at[s, mine_half], core_dev))

    to_x = []
    for s in range(2):
        spread_core[s].wait_recv()
        value = hid[s].reshape(tok_count, tall)
        if s == 0:
            part = jnp.dot(value, w2[...], preferred_element_type=F32)
        else:
            part = lax.dot_general(
                value, w1[...], (((1,), (1,)), ((), ())), preferred_element_type=F32
            )
        xterm[s] = part.reshape(nx, nz, per_x // nz, wide).astype(BF16)
        to_x.append([send(xterm.at[s, k], e1.at[s, k - 1], x_dev(nx - k)) for k in range(1, nx)])

    def grads(s):
        if s == 0:
            left, right = feats[...], hid[1].reshape(tok_count, tall)
        else:
            left, right = hid[0].reshape(tok_count, tall), cots[...]
        full = lax.dot_general(left, right, (((0,), (0,)), ((), ())), preferred_element_type=F32)
        trailing = (cb, rb)[s]
        for place in range(rb * cb):
            a, b = place // trailing, place % trailing
            gdense[s, place] = full[a * BS : (a + 1) * BS, b * BS : (b + 1) * BS].astype(BF16)
        gdense[s, rb * cb] = jnp.zeros((BS, BS), BF16)
        index = (up_idx, down_idx)[s]
        for k in range(slots):
            gout[s, k] = gdense[s, index[0, 0, k]]
        copy = pltpu.make_async_copy(
            gout.at[s], (upg_hbm, downg_hbm)[s].at[0, 0], local_sem.at[2 + s]
        )
        copy.start()
        return copy

    writes = [grads(0)]
    to_z = []
    for s in range(2):
        for copy in to_x[s]:
            copy.wait_recv()
        total = xterm[s, 0].astype(F32)
        for k in range(1, nx):
            total = total + e1[s, k - 1].astype(F32)
        zsum[s] = total.astype(BF16)
        to_z.append([send(zsum.at[s, k], e2.at[s, k - 1], z_dev(nz - k)) for k in range(1, nz)])
    writes.append(grads(1))
    for s, ref in enumerate((out_ref, ing_ref)):
        for copy in to_z[s]:
            copy.wait_recv()
        total = zsum[s, 0].astype(F32)
        for k in range(1, nz):
            total = total + e2[s, k - 1].astype(F32)
        ref[...] = total.astype(BF16)
    for copy in writes:
        copy.wait()
    for copy in started:
        copy.wait_send()


def shards(tokens, up_blocks, up_index, down_blocks, down_index, out_cot):
    own, wide = tokens.shape
    slots = up_blocks.shape[2]
    rb = wide // BS
    nx, ny, nc = NX, NY, NC
    nz = lax.axis_size("col") // nx
    nzh = lax.axis_size("row") // (ny * nc)
    cb = 7
    tall = cb * BS
    tok_count = own * nz * nx
    parts = ny * nc
    rows = tok_count // parts
    n_copies = 2 * (nz - 1 + nx - 1 + 1 + ny - 1 + 1 + ny - 1 + 1 + nx - 1 + nz - 1)
    vmem = pl.BlockSpec(memory_space=pltpu.VMEM)
    smem = pl.BlockSpec(memory_space=pltpu.SMEM)
    hbm = pl.BlockSpec(memory_space=pl.ANY)
    blocks_shape = jax.ShapeDtypeStruct(up_blocks.shape, BF16)
    small = jax.ShapeDtypeStruct((own, wide), BF16)
    return pl.pallas_call(
        functools.partial(body, (nz, nx, nzh, ny, nc, rb, cb, slots)),
        out_shape=(small, small, blocks_shape, blocks_shape),
        in_specs=[vmem, vmem, smem, smem, hbm, hbm],
        out_specs=(vmem, vmem, hbm, hbm),
        scratch_shapes=[
            pltpu.VMEM((slots + 1, BS, BS), BF16),
            pltpu.VMEM((slots + 1, BS, BS), BF16),
            pltpu.VMEM((wide, tall), BF16),
            pltpu.VMEM((tall, wide), BF16),
            pltpu.VMEM((nx, nz, own, wide), BF16),
            pltpu.VMEM((nx, nz, own, wide), BF16),
            pltpu.VMEM((tok_count, wide), BF16),
            pltpu.VMEM((tok_count, wide), BF16),
            pltpu.VMEM((2, parts, rows, tall), BF16),
            pltpu.VMEM((2, ny, rows, tall), BF16),
            pltpu.VMEM((2, ny, rows, tall), BF16),
            pltpu.VMEM((2, ny - 1, rows, tall), BF16),
            pltpu.VMEM((2, rows, tall), BF16),
            pltpu.VMEM((2, rows, tall), BF16),
            pltpu.VMEM((2, parts, rows, tall), BF16),
            pltpu.VMEM((2, nx, nz, own, wide), BF16),
            pltpu.VMEM((2, nx - 1, nz, own, wide), BF16),
            pltpu.VMEM((2, nz, own, wide), BF16),
            pltpu.VMEM((2, nz - 1, own, wide), BF16),
            pltpu.VMEM((2, rb * cb + 1, BS, BS), BF16),
            pltpu.VMEM((2, slots, BS, BS), BF16),
            pltpu.SemaphoreType.DMA((4,)),
            pltpu.SemaphoreType.DMA((n_copies,)),
            pltpu.SemaphoreType.DMA((n_copies,)),
        ],
        compiler_params=pltpu.CompilerParams(
            collective_id=0, has_side_effects=True, vmem_limit_bytes=48 << 20
        ),
    )(tokens, out_cot, up_index, down_index, up_blocks, down_blocks)


def solution(mesh):
    placed = (
        P("col", "row"),
        P("row", "col", None, None, None),
        P("row", "col", None),
        P("row", "col", None, None, None),
        P("row", "col", None),
        P("col", "row"),
    )
    return jax.shard_map(
        shards,
        mesh=mesh,
        in_specs=placed,
        out_specs=(
            P("col", "row"),
            P("col", "row"),
            P("row", "col", None, None, None),
            P("row", "col", None, None, None),
        ),
        check_vma=False,
    )
```

time: 849 us -> 80.3 us (0.09)
  the two profiles are of different devices: /device:TPU:8 before, /device:TPU:1 now
where the time goes in v1:
time: 80.3 us; the launch traced here: 79.4 us
  Pallas kernels  71.6 us (89%)
  local copies, waits for them, and re-layouts  7.15 us (9%)
    pallas_call x1, Pallas kernels, shards(): pl.pallas_call(functools.partial(body, (nz, nx, nzh, ny, nc, rb, cb, slot...  71.6 us
    unnamed x16, local copies, waits for them, and re-layouts  7.15 us

profile of v1, /device:TPU:1, one launch (start us, length us, event | category | flops | bytes accessed | tf_op | source)
XLA Modules:
  0.0 79.4 jit_solution(11875303674256275868)
XLA Ops:
  0.6 0.0 copy-start
  0.6 0.9 %copy-done = bf16[1,1,7,128,128]{4,3,2,1,0:T(8,128)(2,1)S(1)} copy-done((bf16[1,1,7,128,128]{4,3,2,1,0:T(8,128)(2,1)S(1)}, bf16[1,1,7,128,128]{4,3,2,1,0:T(8,128)(2,1)}, u32[]{:S(2)}) %copy-start) | copy-done | bytes 229400
  1.6 0.0 copy-start.1
  1.6 0.9 %copy-done.1 = bf16[1,1,7,128,128]{4,3,2,1,0:T(8,128)(2,1)S(1)} copy-done((bf16[1,1,7,128,128]{4,3,2,1,0:T(8,128)(2,1)S(1)}, bf16[1,1,7,128,128]{4,3,2,1,0:T(8,128)(2,1)}, u32[]{:S(2)}) %copy-start.1) | copy-done | bytes 229400
  2.5 0.0 copy-start.2
  2.5 0.7 copy-done.2
  3.2 0.0 copy-start.3
  3.2 0.7 copy-done.3
  3.9 0.0 copy-start.4
  3.9 0.7 copy-done.4
  4.6 0.0 copy-start.5
  4.6 0.7 copy-done.5
  5.2 71.6 %shard_map.93 = (bf16[8,512]{1,0:T(8,128)(2,1)S(1)}, bf16[8,512]{1,0:T(8,128)(2,1)S(1)}, bf16[1,1,7,128,128]{4,3,2,1,0:T(8,128)(2,1)S(1)}, bf16[1,1,7,128,128]{4,3,2,1,0:T(8,128)(2,1)S(1)}) custom-call(bf16[8,512]{1,0:T(8,128)(2,1)S(1)} %copy-done.2, bf16[8,512]{1,0:T(8,128)(2,1)S(1)} %copy-done.3, s32[1,1,7]{2,1,0:T(1,128)S(1)} %copy-done.4, ...), custom_call_target="tpu_custom_call" | custom-call | tf_op jit(solution)/shard_map/pallas_call | solution.py:281
  76.8 0.6 copy.14
  77.4 0.6 copy.15
  78.0 0.7 copy.16
  78.7 0.7 copy.17
Async XLA Ops:
  0.6 0.9 %copy-start = (bf16[1,1,7,128,128]{4,3,2,1,0:T(8,128)(2,1)S(1)}, bf16[1,1,7,128,128]{4,3,2,1,0:T(8,128)(2,1)}, u32[]{:S(2)}) copy-start(bf16[1,1,7,128,128]{4,3,2,1,0:T(8,128)(2,1)} %up_hbm.1) | copy-start | bytes 688132
  1.6 0.9 %copy-start.1 = (bf16[1,1,7,128,128]{4,3,2,1,0:T(8,128)(2,1)S(1)}, bf16[1,1,7,128,128]{4,3,2,1,0:T(8,128)(2,1)}, u32[]{:S(2)}) copy-start(bf16[1,1,7,128,128]{4,3,2,1,0:T(8,128)(2,1)} %down_hbm.1) | copy-start | bytes 688132
  2.5 0.7 copy-start.2
  3.2 0.7 copy-start.3
  3.9 0.7 copy-start.4
  4.6 0.7 copy-start.5

commit v2 on v1

v2 whole, which is shorter than its diff:
```python
import functools

import jax
import jax.numpy as jnp
from jax import lax
from jax.experimental import pallas as pl
from jax.experimental.pallas import tpu as pltpu
from jax.sharding import PartitionSpec as P

MESH = pl.DeviceIdType.MESH
BF16 = jnp.bfloat16
F32 = jnp.float32

BS = 128
CB = 7
NX = 4
NZ = 8
NY = 4
NC = 2
HZ = NZ // 2
NEAR, FAR = 0, 1

COEF = 0.7978845608
CUBIC = 0.044715


def body(
    tok_hbm,
    cot_hbm,
    up_idx_hbm,
    down_idx_hbm,
    up_hbm,
    down_hbm,
    out_hbm,
    ing_hbm,
    upg_hbm,
    downg_hbm,
    up_blk,
    down_blk,
    w1,
    w2,
    gathered,
    flat,
    term,
    r1,
    half,
    r2,
    share,
    r3,
    hid,
    xterm,
    e1,
    zsum,
    e2,
    gdense,
    gout,
    final,
    up_idx,
    down_idx,
    local_sem,
    send_sem,
    gz_sem,
    gx_sem,
    c1_sem,
    c2_sem,
    c3_sem,
    c4_sem,
    c5_sem,
    e1_sem,
    e2_sem,
):
    own, wide = tok_hbm.shape
    slots = up_hbm.shape[2]
    rb = wide // BS
    cb = CB
    tall = cb * BS
    per_half = HZ * NX * own
    row = lax.axis_index("row")
    col = lax.axis_index("col")
    core = row % NC
    y = (row // NC) % NY
    zh = row // (NC * NY)
    x = col % NX
    z = col // NX
    side = z // HZ
    q = z % HZ
    base = (side * HZ, (1 - side) * HZ)
    near = (side * HZ + q + 1 - 2 * (q % 2), side * HZ + q + 2 - 4 * (q // 2), side * HZ + 3 - q)
    far = tuple(HZ + j - side * (1 + 2 * j) for j in range(HZ))

    def row_of(zh_, y_, core_):
        return (zh_ * NY + y_) * NC + core_

    def z_dev(z_):
        return (row, z_ * NX + x)

    def x_dev(k):
        return (row, z * NX + (x + k) % NX)

    def y_dev(k):
        return (row_of(zh, (y + k) % NY, core), col)

    core_dev = (row_of(zh, y, 1 - core), col)
    zh_dev = (row_of(1 - zh, y, core), col)

    partners = [z_dev(p) for p in far + near] + [x_dev(k) for k in range(1, NX)]
    partners += [y_dev(k) for k in range(1, NY)] + [core_dev, zh_dev]

    barrier = pltpu.get_barrier_semaphore()
    for device in [zh_dev] + partners[:-1]:
        pl.semaphore_signal(barrier, inc=1, device_id=device, device_id_type=MESH)

    started = []

    def send(src, dst, sem, device):
        copy = pltpu.make_async_remote_copy(
            src_ref=src,
            dst_ref=dst,
            send_sem=send_sem.at[len(started)],
            recv_sem=sem,
            device_id=device,
            device_id_type=MESH,
        )
        copy.start()
        started.append(copy)

    def arrived(dst, sem):
        pltpu.make_async_remote_copy(
            src_ref=dst,
            dst_ref=dst,
            send_sem=send_sem.at[0],
            recv_sem=sem,
            device_id=core_dev,
            device_id_type=MESH,
        ).wait_recv()

    def load(at, src, dst):
        copy = pltpu.make_async_copy(src, dst, local_sem.at[at])
        copy.start()
        return copy

    tok_load = load(0, tok_hbm, gathered.at[0, z, 0])
    cot_load = load(1, cot_hbm, gathered.at[0, z, 1])
    up_idx_load = load(2, up_idx_hbm, up_idx)
    down_idx_load = load(3, down_idx_hbm, down_idx)
    up_load = load(4, up_hbm.at[0, 0], up_blk.at[pl.ds(0, slots)])
    down_load = load(5, down_hbm.at[0, 0], down_blk.at[pl.ds(0, slots)])

    for idx_load, blk_load, blk, index, dense, leading, trailing in (
        (up_idx_load, up_load, up_blk, up_idx, w1, rb, cb),
        (down_idx_load, down_load, down_blk, down_idx, w2, cb, rb),
    ):
        blk[slots] = jnp.zeros((BS, BS), BF16)
        idx_load.wait()
        blk_load.wait()
        entries = [index[0, 0, k] for k in range(slots)]
        for place in range(leading * trailing):
            slot = jnp.int32(slots)
            for k in range(slots):
                slot = jnp.where(entries[k] == place, jnp.int32(k), slot)
            a, b = place // trailing, place % trailing
            dense[a * BS : (a + 1) * BS, b * BS : (b + 1) * BS] = blk[slot]

    tok_load.wait()
    cot_load.wait()
    with jax.named_scope("w_barrier"):
        pl.semaphore_wait(barrier, len(partners))

    for p in far[::-1] + near[::-1]:
        send(gathered.at[0, z], gathered.at[0, z], gz_sem.at[z], z_dev(p))

    def forward(p):
        for k in range(1, NX):
            send(gathered.at[0, p], gathered.at[k, p], gx_sem.at[k - 1, p], x_dev(k))

    forward(z)
    for j, places in ((NEAR, near), (FAR, far)):
        for p in places:
            with jax.named_scope(f"w_gz{j}"):
                arrived(gathered.at[0, p], gz_sem.at[p])
            forward(p)

    def terms(j):
        with jax.named_scope(f"w_gx{j}"):
            for k in range(1, NX):
                for i in range(HZ):
                    p = base[j] + i
                    arrived(gathered.at[k, p], gx_sem.at[k - 1, p])
        for s in range(2):
            for k in range(NX):
                flat[s, j, k * HZ * own : (k + 1) * HZ * own, :] = (
                    gathered[k, pl.ds(base[j], HZ), s]
                    .astype(F32)
                    .reshape(HZ * own, wide)
                    .astype(BF16)
                )
            if s == 0:
                value = jnp.dot(flat[s, j], w1[...], preferred_element_type=F32)
            else:
                value = lax.dot_general(
                    flat[s, j], w2[...], (((1,), (1,)), ((), ())), preferred_element_type=F32
                )
            term[j, s] = value.astype(BF16).reshape(term.shape[2:])
            send(term.at[j, s, pl.ds((1 - core) * NY, NY)], r1.at[j, s], c1_sem.at[j, s], core_dev)

    def to_y(j, s):
        with jax.named_scope(f"w_c1_{j}{s}"):
            arrived(r1.at[j, s], c1_sem.at[j, s])
        half[j, s] = (
            term[j, s, pl.ds(core * NY, NY)].astype(F32) + r1[j, s].astype(F32)
        ).astype(BF16)
        for k in range(1, NY):
            send(half.at[j, s, (y + k) % NY], r2.at[j, s, k - 1], c2_sem.at[j, s, k - 1], y_dev(k))

    def to_zh(j, s):
        with jax.named_scope(f"w_c2_{j}{s}"):
            for k in range(1, NY):
                arrived(r2.at[j, s, k - 1], c2_sem.at[j, s, k - 1])
        total = half[j, s, y].astype(F32)
        for k in range(1, NY):
            total = total + r2[j, s, k - 1].astype(F32)
        share[j, s] = total.astype(BF16)
        send(share.at[j, s], r3.at[j, s], c3_sem.at[j, s], zh_dev)

    mine = core * NY + y

    def shared(j, s):
        with jax.named_scope(f"w_c3_{j}{s}"):
            arrived(r3.at[j, s], c3_sem.at[j, s])
        return share[j, s].astype(F32) + r3[j, s].astype(F32)

    def spread(j, s):
        if s == 0:
            v = shared(j, 0)
            t = jnp.tanh(COEF * (v + CUBIC * v * v * v))
            hid[j, s, mine] = (0.5 * v * (1.0 + t)).astype(BF16)
        else:
            act = shared(j, 1)
            v = share[j, 0].astype(F32) + r3[j, 0].astype(F32)
            t = jnp.tanh(COEF * (v + CUBIC * v * v * v))
            slope = 0.5 * (1.0 + t) + 0.5 * v * (1.0 - t * t) * COEF * (1.0 + 3.0 * CUBIC * v * v)
            hid[j, s, mine] = (act * slope).astype(BF16)
        for k in range(1, NY):
            send(hid.at[j, s, mine], hid.at[j, s, mine], c4_sem.at[j, s, k - 1], y_dev(k))

    def to_core(j, s):
        with jax.named_scope(f"w_c4_{j}{s}"):
            for k in range(1, NY):
                place = core * NY + (y - k) % NY
                arrived(hid.at[j, s, place], c4_sem.at[j, s, k - 1])
        places = pl.ds(core * NY, NY)
        send(hid.at[j, s, places], hid.at[j, s, places], c5_sem.at[j, s], core_dev)

    def to_x(j, s):
        with jax.named_scope(f"w_c5_{j}{s}"):
            arrived(hid.at[j, s, pl.ds((1 - core) * NY, NY)], c5_sem.at[j, s])
        value = hid[j, s].reshape(per_half, tall)
        if s == 0:
            part = jnp.dot(value, w2[...], preferred_element_type=F32)
        else:
            part = lax.dot_general(
                value, w1[...], (((1,), (1,)), ((), ())), preferred_element_type=F32
            )
        xterm[j, s] = part.reshape(NX, HZ, own, wide).astype(BF16)
        for k in range(1, NX):
            send(xterm.at[j, s, k], e1.at[j, s, k - 1], e1_sem.at[j, s, k - 1], x_dev(NX - k))

    def to_z(j, s):
        with jax.named_scope(f"w_e1_{j}{s}"):
            for k in range(1, NX):
                arrived(e1.at[j, s, k - 1], e1_sem.at[j, s, k - 1])
        total = xterm[j, s, 0].astype(F32)
        for k in range(1, NX):
            total = total + e1[j, s, k - 1].astype(F32)
        zsum[j, s] = total.astype(BF16)
        for p in (near, far)[j][::-1]:
            send(zsum.at[j, s, p % HZ], e2.at[s, z], e2_sem.at[s, z], z_dev(p))
        if j == NEAR:
            e2[s, z] = zsum[j, s, q]

    def grads(s):
        if s == 0:
            left = flat[0].reshape(2 * per_half, wide)
            right = hid[:, 1].reshape(2 * per_half, tall)
        else:
            left = hid[:, 0].reshape(2 * per_half, tall)
            right = flat[1].reshape(2 * per_half, wide)
        full = lax.dot_general(left, right, (((0,), (0,)), ((), ())), preferred_element_type=F32)
        trailing = (cb, rb)[s]
        for place in range(rb * cb):
            a, b = place // trailing, place % trailing
            gdense[s, place] = full[a * BS : (a + 1) * BS, b * BS : (b + 1) * BS].astype(BF16)
        gdense[s, rb * cb] = jnp.zeros((BS, BS), BF16)
        index = (up_idx, down_idx)[s]
        for k in range(slots):
            gout[s, k] = gdense[s, index[0, 0, k]]
        return load(6 + s, gout.at[s], (upg_hbm, downg_hbm)[s].at[0, 0])

    terms(NEAR)
    to_y(NEAR, 0)
    to_y(NEAR, 1)
    terms(FAR)
    to_y(FAR, 0)
    to_y(FAR, 1)
    to_zh(NEAR, 0)
    to_zh(NEAR, 1)
    to_zh(FAR, 0)
    to_zh(FAR, 1)
    spread(NEAR, 0)
    spread(NEAR, 1)
    to_core(NEAR, 0)
    spread(FAR, 0)
    to_core(NEAR, 1)
    to_x(NEAR, 0)
    spread(FAR, 1)
    to_x(NEAR, 1)
    to_core(FAR, 0)
    to_x(FAR, 0)
    to_core(FAR, 1)
    to_x(FAR, 1)
    to_z(FAR, 0)
    with jax.named_scope("grads1"):
        writes = [grads(1)]
    to_z(FAR, 1)
    to_z(NEAR, 0)
    to_z(NEAR, 1)
    with jax.named_scope("grads0"):
        writes.append(grads(0))
    for s, ref in enumerate((out_hbm, ing_hbm)):
        with jax.named_scope(f"w_e2_{s}"):
            for p in near + far:
                arrived(e2.at[s, p], e2_sem.at[s, p])
        total = e2[s, 0].astype(F32)
        for p in range(1, NZ):
            total = total + e2[s, p].astype(F32)
        final[s] = total.astype(BF16)
        writes.append(load(8 + s, final.at[s], ref))
    for copy in writes:
        copy.wait()
    for copy in started:
        copy.wait_send()


def hand_over(*refs):
    sources, targets, bounce, sem = refs[:4], refs[4:8], refs[8:12], refs[12]
    order = (2, 3, 0, 1)
    loads = {i: pltpu.make_async_copy(sources[i], bounce[i], sem.at[0, i]) for i in order}
    stores = {i: pltpu.make_async_copy(bounce[i], targets[i], sem.at[1, i]) for i in order}
    for i in order:
        loads[i].start()
    for i in order:
        loads[i].wait()
        stores[i].start()
    for i in order:
        stores[i].wait()


def shards(tokens, up_blocks, up_index, down_blocks, down_index, out_cot):
    own, wide = tokens.shape
    slots = up_blocks.shape[2]
    rb = wide // BS
    tall = CB * BS
    parts = NC * NY
    rows = HZ * NX * own // parts
    n_copies = NZ - 1 + NZ * (NX - 1) + 4 * (1 + NY - 1 + 1 + NY - 1 + 1 + NX - 1) + 2 * (NZ - 1)
    hbm = pl.BlockSpec(memory_space=pltpu.HBM)
    blocks_shape = jax.ShapeDtypeStruct(up_blocks.shape, BF16)
    small = jax.ShapeDtypeStruct((own, wide), BF16)
    dma = pltpu.SemaphoreType.DMA
    results = pl.pallas_call(
        body,
        out_shape=(small, small, blocks_shape, blocks_shape),
        in_specs=[hbm] * 6,
        out_specs=(hbm,) * 4,
        scratch_shapes=[
            pltpu.VMEM((slots + 1, BS, BS), BF16),
            pltpu.VMEM((slots + 1, BS, BS), BF16),
            pltpu.VMEM((wide, tall), BF16),
            pltpu.VMEM((tall, wide), BF16),
            pltpu.VMEM((NX, NZ, 2, own, wide), BF16),
            pltpu.VMEM((2, 2, HZ * NX * own, wide), BF16),
            pltpu.VMEM((2, 2, parts, rows, tall), BF16),
            pltpu.VMEM((2, 2, NY, rows, tall), BF16),
            pltpu.VMEM((2, 2, NY, rows, tall), BF16),
            pltpu.VMEM((2, 2, NY - 1, rows, tall), BF16),
            pltpu.VMEM((2, 2, rows, tall), BF16),
            pltpu.VMEM((2, 2, rows, tall), BF16),
            pltpu.VMEM((2, 2, parts, rows, tall), BF16),
            pltpu.VMEM((2, 2, NX, HZ, own, wide), BF16),
            pltpu.VMEM((2, 2, NX - 1, HZ, own, wide), BF16),
            pltpu.VMEM((2, 2, HZ, own, wide), BF16),
            pltpu.VMEM((2, NZ, own, wide), BF16),
            pltpu.VMEM((2, rb * CB + 1, BS, BS), BF16),
            pltpu.VMEM((2, slots, BS, BS), BF16),
            pltpu.VMEM((2, own, wide), BF16),
            pltpu.SMEM(up_index.shape, jnp.int32),
            pltpu.SMEM(down_index.shape, jnp.int32),
            dma((10,)),
            dma((n_copies,)),
            dma((NZ,)),
            dma((NX - 1, NZ)),
            dma((2, 2)),
            dma((2, 2, NY - 1)),
            dma((2, 2)),
            dma((2, 2, NY - 1)),
            dma((2, 2)),
            dma((2, 2, NX - 1)),
            dma((2, NZ)),
        ],
        compiler_params=pltpu.CompilerParams(collective_id=0, has_side_effects=True),
    )(tokens, out_cot, up_index, down_index, up_blocks, down_blocks)
    return pl.pallas_call(
        hand_over,
        out_shape=(small, small, blocks_shape, blocks_shape),
        in_specs=[hbm] * 4,
        out_specs=(hbm,) * 4,
        scratch_shapes=[
            pltpu.VMEM(small.shape, BF16),
            pltpu.VMEM(small.shape, BF16),
            pltpu.VMEM(blocks_shape.shape, BF16),
            pltpu.VMEM(blocks_shape.shape, BF16),
            dma((2, 4)),
        ],
    )(*results)


def solution(mesh):
    placed = (
        P("col", "row"),
        P("row", "col", None, None, None),
        P("row", "col", None),
        P("row", "col", None, None, None),
        P("row", "col", None),
        P("col", "row"),
    )
    return jax.shard_map(
        shards,
        mesh=mesh,
        in_specs=placed,
        out_specs=(
            P("col", "row"),
            P("col", "row"),
            P("row", "col", None, None, None),
            P("row", "col", None, None, None),
        ),
        check_vma=False,
    )
```

time: 80.3 us -> 69.3 us (0.86)
  local copies, waits for them, and re-layouts: 7.15 us -> 0 us
  Pallas kernels: 71.6 us -> 68.5 us
    unnamed x16 -> x0, local copies, waits for them, and re-layouts: 7.15 us -> none
    pallas_call x1 -> x2, Pallas kernels: 71.6 us -> 68.5 us  [the longest x1 66.7 us: shards(): pl.pallas_call(body, out_shape=(small, small, blocks_shape, blocks_shape)...]
where the time goes in v2:
time: 69.3 us; the launch traced here: 69.1 us
  Pallas kernels  68.5 us (99%)
    pallas_call x1, Pallas kernels, shards(): pl.pallas_call(body, out_shape=(small, small, blocks_shape, blocks_shape)...  66.7 us
    pallas_call x1, Pallas kernels, shards(): pl.pallas_call(hand_over, out_shape=(small, small, blocks_shape, blocks_s...  1.81 us

profile of v2, /device:TPU:1, one launch (start us, length us, event | category | flops | bytes accessed | tf_op | source)
XLA Modules:
  0.0 69.1 jit_solution(6910971314025392286)
XLA Ops:
  0.6 66.7 %shard_map.93 = (bf16[8,512]{1,0:T(8,128)(2,1)}, bf16[8,512]{1,0:T(8,128)(2,1)}, bf16[1,1,7,128,128]{4,3,2,1,0:T(8,128)(2,1)}, bf16[1,1,7,128,128]{4,3,2,1,0:T(8,128)(2,1)}) custom-call(bf16[8,512]{1,0:T(8,128)(2,1)} %tok_hbm.1, bf16[8,512]{1,0:T(8,128)(2,1)} %cot_hbm.1, s32[1,1,7]{2,1,0:T(1,128)} %up_idx_hbm.1, s32[1,1,7]{2,1,0:T(1,128)} %down_idx_hbm.1, ...), custom_call_target="tpu_custom_call" | custom-call | tf_op jit(solution)/shard_map/pallas_call | solution.py:370
  67.3 1.8 %shard_map.94 = (bf16[8,512]{1,0:T(8,128)(2,1)}, bf16[8,512]{1,0:T(8,128)(2,1)}, bf16[1,1,7,128,128]{4,3,2,1,0:T(8,128)(2,1)}, bf16[1,1,7,128,128]{4,3,2,1,0:T(8,128)(2,1)}) custom-call(bf16[8,512]{1,0:T(8,128)(2,1)} %get-tuple-element.8.refs_0_, bf16[8,512]{1,0:T(8,128)(2,1)} %get-tuple-element.9.refs_1_, ...), custom_call_target="tpu_custom_call" | custom-call | tf_op jit(solution)/shard_map/pallas_call | solution.py:412
